TPU v7x, 256 devices: a whole 4x4x8 slice. The times are simulated.
256 devices in a mesh: batch: 2 (over z_lo), seq: 128 (over z_hi, y, x, core).
Axes of the slice: x: 4, y: 4, z: 8 (z_hi: 4, z_lo: 2; z = z_hi * 2 + z_lo), core: 2. Of those that a mesh axis runs over, the one named last changes fastest.
Arguments:
- signal: bfloat16 [2, 262144, 384], P('batch', 'seq'), may hold values from -6 to 6
- conv_weight: float32 [4, 384], replicated, may hold values from -2.5 to 2.5
- first_factor: bfloat16 [512, 512, 512], P('seq'), may hold values from -0.25 to 0.25
- second_factor: bfloat16 [512, 512, 512], P('seq'), may hold values from -0.25 to 0.25
- grad_output: bfloat16 [2, 262144, 384], P('batch', 'seq'), may hold values from -3 to 3
Outputs:
- grad_signal: bfloat16 [2, 262144, 384], P('batch', 'seq')
- grad_first: bfloat16 [512, 512, 512], P('seq', 'batch')
- grad_second: bfloat16 [512, 512, 512], P('seq', 'batch')
All inputs are finite; a program needn't handle non-finite values.
Results may differ from a plain program's by a relative error of at most 0.0065.
Values may be sent and summed in bfloat16 or wider, within the bound.
A program may use at most 128 MiB of HBM per device.

v0:
```python
import jax
import jax.numpy as jnp
from jax import lax
from jax.sharding import PartitionSpec as P


def passed_along(value, axis, steps):
    count = lax.axis_size(axis)
    initial, last = (max(0, -steps), min(count, count - steps))
    return lax.ppermute(value, axis, [(source, source + steps) for source in range(initial, last)])


def body(signal, conv_weight, first_factor, second_factor, grad_output):
    seq_count, tok_rows, channels = signal.shape
    blocks = first_factor.shape[0]
    block_order = first_factor.shape[1]
    col_blocks = second_factor.shape[0]
    block_count = second_factor.shape[1]
    tap_count = conv_weight.shape[0]
    previous = passed_along(signal[:, tok_rows - (tap_count - 1) :, :], "seq", 1)
    padded_in = jnp.concatenate([previous, signal], axis=1).astype(jnp.float32)
    conv_out = sum(
        (
            conv_weight[r][None, None, :]
            * padded_in[:, tap_count - 1 - r : tap_count - 1 - r + tok_rows, :]
            for r in range(tap_count)
        )
    )
    gate_val = jax.nn.sigmoid(conv_out)
    hidden = (conv_out * gate_val).astype(jnp.bfloat16)
    hidden_blocks = hidden.reshape(seq_count, blocks, block_order, channels)
    mixed = jnp.einsum(
        "ikj,sijd->sikd", first_factor, hidden_blocks, preferred_element_type=jnp.float32
    ).astype(jnp.bfloat16)
    columns = lax.all_to_all(mixed, "seq", split_axis=2, concat_axis=1, tiled=True)
    upstream = grad_output.reshape(seq_count, col_blocks, block_count, channels)
    grad_mixed = jnp.einsum(
        "kmi,skmd->sikd", second_factor, upstream, preferred_element_type=jnp.float32
    ).astype(jnp.bfloat16)
    grad_second = jnp.einsum(
        "skmd,sikd->kmi", upstream, columns, preferred_element_type=jnp.float32
    )
    grad_rows = lax.all_to_all(grad_mixed, "seq", split_axis=1, concat_axis=2, tiled=True)
    grad_hidden = jnp.einsum(
        "ikj,sikd->sijd", first_factor, grad_rows, preferred_element_type=jnp.float32
    ).reshape(seq_count, tok_rows, channels)
    grad_conv = (grad_hidden * gate_val * (1.0 + conv_out * (1.0 - gate_val))).astype(jnp.bfloat16)
    following = passed_along(grad_conv[:, : tap_count - 1, :], "seq", -1)
    extended = jnp.concatenate([grad_conv, following], axis=1).astype(jnp.float32)
    grad_signal = sum(
        (conv_weight[r][None, None, :] * extended[:, r : r + tok_rows, :] for r in range(tap_count))
    ).astype(jnp.bfloat16)
    grad_first = jnp.einsum(
        "sikd,sijd->ikj", grad_rows, hidden_blocks, preferred_element_type=jnp.float32
    )
    total_first, total_second = (
        lax.psum(grad_first.astype(jnp.bfloat16), "batch").astype(jnp.float32),
        lax.psum(grad_second.astype(jnp.bfloat16), "batch").astype(jnp.float32),
    )
    batch_index = lax.axis_index("batch")
    half_first = total_first.shape[1] // lax.axis_size("batch")
    half_second = total_second.shape[1] // lax.axis_size("batch")
    share_first = lax.dynamic_slice_in_dim(total_first, batch_index * half_first, half_first, 1)
    share_second = lax.dynamic_slice_in_dim(total_second, batch_index * half_second, half_second, 1)
    return (grad_signal, share_first.astype(jnp.bfloat16), share_second.astype(jnp.bfloat16))


def solution(mesh):
    placed = (
        P("batch", "seq", None),
        P(),
        P("seq", None, None),
        P("seq", None, None),
        P("batch", "seq", None),
    )
    return jax.shard_map(
        body,
        mesh=mesh,
        in_specs=placed,
        out_specs=(P("batch", "seq", None), P("seq", "batch", None), P("seq", "batch", None)),
        check_vma=False,
    )
```

profile of v0, /device:TPU:1, one launch (start us, length us, event | category | flops | bytes accessed | tf_op | source)
XLA Modules:
  0.0 269.5 jit_solution(10913673899404368837)
XLA Ops:
  7.2 4.4 %fusion.9 = bf16[1,512,4,384]{1,3,2,0:T(8,128)(2,1)} fusion(bf16[4,512,384]{2,1,0:T(8,128)(2,1)} %bitcast.39, bf16[4,512,512]{2,1,0:T(8,128)(2,1)} %param.8), kind=kOutput, calls=%fused_computation.29 | convolution fusion | flops 806092800 | bytes 5242880 | tf_op jit(solution)/shard_map/kmi,skmd->sikd/dot_general | solution.py:37
  11.6 3.8 %copy.25 = bf16[1,512,4,384]{3,2,0,1:T(4,128)(2,1)} copy(bf16[1,512,4,384]{1,3,2,0:T(8,128)(2,1)} %fusion.9) | data formatting | bytes 3145728 | tf_op jit(solution)/shard_map/convert_element_type | solution.py:39
  15.3 16.9 %all-to-all-start = ((bf16[1,512,4,384]{3,2,0,1:T(4,128)(2,1)}), bf16[1,512,4,384]{3,2,0,1:T(4,128)(2,1)}, u32[]{:S(2)}, u32[]{:S(2)}) async-start(bf16[1,512,4,384]{3,2,0,1:T(4,128)(2,1)} %copy.25), calls=%async_computation | async-start | bytes 3145728 | tf_op jit(solution)/shard_map/all_to_all | solution.py:43
  32.3 0.7 slice.47
  33.0 3.5 %collective-permute-start = (bf16[1,3,384]{2,1,0:T(4,128)(2,1)S(1)}, bf16[1,3,384]{2,1,0:T(4,128)(2,1)S(1)}, u32[]{:S(2)}, u32[]{:S(2)}) collective-permute-start(bf16[1,3,384]{2,1,0:T(4,128)(2,1)S(1)} %slice.47), channel_id=1, source_target_pairs={{0,1},{1,2},{2,3},{3,4},{4,5},{5,6},{6,7},{7,8},{8,9},{9,10},{10,1... | collective-permute-start | bytes 6920 | tf_op jit(solution)/shard_map/ppermute | solution.py:10
  36.6 0.7 collective-permute-done
  37.2 1.7 maximum_convert_fusion
  39.0 3.1 %multiply_convert_fusion = (bf16[1,2048,384]{2,1,0:T(8,128)(2,1)S(1)}, f32[1,2048,384]{2,1,0:T(8,128)}) fusion(f32[1,2051,384]{2,1,0:T(8,128)S(1)} %maximum_convert_fusion, f32[384]{0:T(512)S(1)} %get-tuple-element.14, f32[384]{0:T(512)S(1)} %get-tuple-element.15, f32[384]{0:T(512)S(1)} %get-tuple-element.13, f32[384]{0:T(512)S(1)} %get-tuple-element.12), kind=kLoop, calls=%fused_computation.18 | loop fusion | flops 9437184 | bytes 17307648 | tf_op jit(solution)/shard_map/convert_element_type | solution.py:30
  42.1 1.2 copy-done.3
  43.3 2.3 fusion.10
  45.6 3.8 %copy.31 = bf16[1,4,512,384]{3,1,0,2:T(4,128)(2,1)} copy(bf16[1,4,512,384]{2,3,1,0:T(8,128)(2,1)} %fusion.10) | data formatting | bytes 3145728 | tf_op jit(solution)/shard_map/convert_element_type | solution.py:34
  49.4 23.6 %all-to-all-done = bf16[1,512,4,384]{3,2,0,1:T(4,128)(2,1)} async-done(((bf16[1,512,4,384]{3,2,0,1:T(4,128)(2,1)}), bf16[1,512,4,384]{3,2,0,1:T(4,128)(2,1)}, u32[]{:S(2)}, u32[]{:S(2)}) %all-to-all-start) | async-done | bytes 1572896 | tf_op jit(solution)/shard_map/all_to_all | solution.py:43
  73.0 17.0 %all-to-all-start.1 = ((bf16[1,4,512,384]{3,1,0,2:T(4,128)(2,1)}), bf16[1,4,512,384]{3,1,0,2:T(4,128)(2,1)}, u32[]{:S(2)}, u32[]{:S(2)}) async-start(bf16[1,4,512,384]{3,1,0,2:T(4,128)(2,1)} %copy.31), calls=%async_computation.1 | async-start | bytes 3145728 | tf_op jit(solution)/shard_map/all_to_all | solution.py:35
  90.2 2.1 copy.26
  92.4 1.1 copy-done.2
  93.5 2.6 convolution_convert_fusion
  96.1 30.5 %all-to-all-done.1 = bf16[1,4,512,384]{3,1,0,2:T(4,128)(2,1)} async-done(((bf16[1,4,512,384]{3,1,0,2:T(4,128)(2,1)}), bf16[1,4,512,384]{3,1,0,2:T(4,128)(2,1)}, u32[]{:S(2)}, u32[]{:S(2)}) %all-to-all-start.1) | async-done | bytes 1572896 | tf_op jit(solution)/shard_map/all_to_all | solution.py:35
  126.6 3.1 %copy.32 = bf16[1,128,4,4,384]{4,2,1,3,0:T(4,128)(2,1)} copy(bf16[1,128,4,4,384]{4,2,3,1,0:T(4,128)(2,1)} %bitcast.13) | data formatting | bytes 3145728 | tf_op jit(solution)/shard_map/all_to_all | solution.py:35
  129.7 3.7 %reshape.110 = bf16[512,4,384]{2,0,1:T(8,128)(2,1)} reshape(bf16[1,128,4,4,384]{4,2,1,3,0:T(4,128)(2,1)} %copy.32) | data formatting | bytes 3145728 | tf_op jit(solution)/shard_map/reshape.23
  133.4 4.6 %convert_bitcast_fusion = bf16[4,512,512]{1,2,0:T(8,128)(2,1)} fusion(bf16[512,4,384]{2,0,1:T(8,128)(2,1)} %reshape.110, bf16[4,512,384]{2,1,0:T(8,128)(2,1)} %bitcast.40), kind=kOutput, calls=%fused_computation.21 | convolution fusion | flops 806354944 | bytes 5242880 | tf_op jit(solution)/shard_map/skmd,sikd->kmi/dot_general | solution.py:40
  138.0 4.1 %convolution_bitcast_fusion = f32[1,4,512,384]{2,3,1,0:T(8,128)} fusion(bf16[4,512,512]{2,1,0:T(8,128)(2,1)S(1)} %copy-done, bf16[4,512,384]{2,0,1:T(4,128)(2,1)} %bitcast.42), kind=kOutput, calls=%fused_computation.24 | convolution fusion | flops 805306368 | bytes 6815744 | tf_op jit(solution)/shard_map/ikj,sikd->sijd/dot_general | solution.py:44
  142.2 3.6 %copy.28 = f32[1,4,512,384]{3,2,1,0:T(8,128)} copy(f32[1,4,512,384]{2,3,1,0:T(8,128)} %convolution_bitcast_fusion) | data formatting | bytes 6291456 | tf_op jit(solution)/shard_map/ikj,sikd->sijd/transpose | solution.py:44
  145.7 4.0 %fusion.8 = bf16[1,2048,384]{2,1,0:T(8,128)(2,1)S(1)} fusion(f32[1,4,512,384]{3,2,1,0:T(8,128)} %copy.28, f32[1,2048,384]{2,1,0:T(8,128)} %get-tuple-element.19), kind=kLoop, calls=%fused_computation.17 | loop fusion | flops 7077888 | bytes 7864320 | tf_op jit(solution)/shard_map/convert_element_type | solution.py:47
  149.7 1.1 copy-done.1
  150.8 10.2 %collective-permute-start.1 = (bf16[1,3,384]{2,1,0:T(4,128)(2,1)S(1)}, bf16[1,3,384]{2,1,0:T(4,128)(2,1)S(1)}, u32[]{:S(2)}, u32[]{:S(2)}) collective-permute-start(bf16[1,3,384]{2,1,0:T(4,128)(2,1)S(1)} %slice.64), channel_id=1, source_target_pairs={{1,0},{2,1},{3,2},{4,3},{5,4},{6,5},{7,6},{8,7},{9,8},{10,9},{11,1... | collective-permute-start | bytes 6920 | tf_op jit(solution)/shard_map/ppermute | solution.py:10
  161.1 0.8 collective-permute-done.1
  161.9 1.6 maximum_convert_fusion.1
  163.5 2.5 fusion.1
  166.1 91.7 %all-reduce.3.cloned.1.call-done = (bf16[4,512,512]{2,1,0:T(8,128)(2,1)}, bf16[4,512,512]{1,2,0:T(8,128)(2,1)}) async-done(((bf16[4,512,512]{2,1,0:T(8,128)(2,1)}, bf16[4,512,512]{1,2,0:T(8,128)(2,1)}), (bf16[4,512,512]{2,1,0:T(8,128)(2,1)}, bf16[4,512,512]{1,2,0:T(8,128)(2,1)})) %all-reduce.3.cloned.1.call-update) | async-done | bytes 4194320 | tf_op jit(solution)/shard_map/psum | solution.py:57
  257.8 1.3 convert_convert_fusion
  259.1 1.3 copy.33
  260.4 2.3 convert_convert_fusion.1
  (13 shorter events, 0.3 us)
Async XLA Ops:
  7.2 36.1 %copy-start = (bf16[4,512,512]{2,1,0:T(8,128)(2,1)S(1)}, bf16[4,512,512]{2,1,0:T(8,128)(2,1)}, u32[]{:S(2)}) copy-start(bf16[4,512,512]{2,1,0:T(8,128)(2,1)} %param.7) | copy-start | bytes 6291460
  15.3 21.2 %copy-start.5 = (f32[4,384]{1,0:T(4,128)S(1)}, f32[4,384]{1,0:T(4,128)}, u32[]{:S(2)}) copy-start(f32[4,384]{1,0:T(4,128)} %param.6) | copy-start | bytes 18436
  15.3 57.7 %all-to-all-start = ((bf16[1,512,4,384]{3,2,0,1:T(4,128)(2,1)}), bf16[1,512,4,384]{3,2,0,1:T(4,128)(2,1)}, u32[]{:S(2)}, u32[]{:S(2)}) async-start(bf16[1,512,4,384]{3,2,0,1:T(4,128)(2,1)} %copy.25), calls=%async_computation | async-start | bytes 3145728 | tf_op jit(solution)/shard_map/all_to_all | solution.py:43
  33.0 4.3 %collective-permute-start = (bf16[1,3,384]{2,1,0:T(4,128)(2,1)S(1)}, bf16[1,3,384]{2,1,0:T(4,128)(2,1)S(1)}, u32[]{:S(2)}, u32[]{:S(2)}) collective-permute-start(bf16[1,3,384]{2,1,0:T(4,128)(2,1)S(1)} %slice.47), channel_id=1, source_target_pairs={{0,1},{1,2},{2,3},{3,4},{4,5},{5,6},{6,7},{7,8},{8,9},{9,10},{10,1... | collective-permute-start | bytes 6920 | tf_op jit(solution)/shard_map/ppermute | solution.py:10
  42.1 1.2 copy-start.3
  73.0 53.6 %all-to-all-start.1 = ((bf16[1,4,512,384]{3,1,0,2:T(4,128)(2,1)}), bf16[1,4,512,384]{3,1,0,2:T(4,128)(2,1)}, u32[]{:S(2)}, u32[]{:S(2)}) async-start(bf16[1,4,512,384]{3,1,0,2:T(4,128)(2,1)} %copy.31), calls=%async_computation.1 | async-start | bytes 3145728 | tf_op jit(solution)/shard_map/all_to_all | solution.py:35
  90.0 167.8 %all-reduce.3.cloned.1.call-start = ((), (), s32[]{:S(2)}) async-start(), calls=%async_computation.2 | async-start | bytes 8388608 | tf_op jit(solution)/shard_map/psum | solution.py:57
  90.2 3.3 %copy-start.4 = (bf16[1,2048,384]{2,1,0:T(8,128)(2,1)S(1)}, bf16[1,2048,384]{2,1,0:T(8,128)(2,1)}, u32[]{:S(2)}) copy-start(bf16[1,2048,384]{2,1,0:T(8,128)(2,1)} %copy-done.3) | copy-start | bytes 4718596
  92.4 1.1 copy-start.2
  149.7 1.1 copy-start.1
  150.8 11.1 %collective-permute-start.1 = (bf16[1,3,384]{2,1,0:T(4,128)(2,1)S(1)}, bf16[1,3,384]{2,1,0:T(4,128)(2,1)S(1)}, u32[]{:S(2)}, u32[]{:S(2)}) collective-permute-start(bf16[1,3,384]{2,1,0:T(4,128)(2,1)S(1)} %slice.64), channel_id=1, source_target_pairs={{1,0},{2,1},{3,2},{4,3},{5,4},{6,5},{7,6},{8,7},{9,8},{10,9},{11,1... | collective-permute-start | bytes 6920 | tf_op jit(solution)/shard_map/ppermute | solution.py:10
Sparse Core Ops, SparseCore 0:
  138.2 119.5 all-reduce.2
where the time goes:
time: 270 us
  waiting for transfers between devices  147 us (54%)
  starting transfers between devices  47.9 us (18%)
  local copies, waits for them, and re-layouts  25.7 us (10%)
  matrix products  18 us (7%)
  other arithmetic  16.5 us (6%)
  between operations  14.1 us (5%)
    psum x1, waiting for transfers between devices, body(): lax.psum(grad_first.astype(jnp.bfloat16), 'batch').astype(jnp.float32)  91.7 us
    all_to_all x1, waiting for transfers between devices, body(): lax.all_to_all(mixed, 'seq', split_axis=2, concat_axis=1, tiled=True)  30.5 us
    all_to_all x1, waiting for transfers between devices, body(): lax.all_to_all(grad_mixed, 'seq', split_axis=1, concat_axis=2, tiled=True)  23.6 us
    all_to_all x1, starting transfers between devices, body(): lax.all_to_all(mixed, 'seq', split_axis=2, concat_axis=1, tiled=True)  17 us
    all_to_all x1, starting transfers between devices, body(): lax.all_to_all(grad_mixed, 'seq', split_axis=1, concat_axis=2, tiled=True)  16.9 us
    ppermute x2, starting transfers between devices, passed_along(): lax.ppermute(value, axis, [(source, source + steps) for source in range(i...  13.8 us
  transfers between devices with their start and end apart: 5, of which 5 were waited for; matrix products, arithmetic and copies ran while one was open for 12% of the time, Pallas kernels for 0%

commit v1 on v0

--- a/solution.py
+++ b/solution.py
@@ -54,7 +54,9 @@
         "sikd,sijd->ikj", grad_rows, hidden_blocks, preferred_element_type=jnp.float32
     )
     total_first, total_second = (
-        lax.psum(grad_first.astype(jnp.bfloat16), "batch").astype(jnp.float32),
+        jnp.sum(lax.all_gather(grad_first.astype(jnp.bfloat16), "batch"), axis=0).astype(
+            jnp.float32
+        ),
         lax.psum(grad_second.astype(jnp.bfloat16), "batch").astype(jnp.float32),
     )
     batch_index = lax.axis_index("batch")

time: 270 us -> 269 us (level)
  starting transfers between devices: 47.9 us -> 36.2 us
  other arithmetic: 16.5 us -> 21.5 us
  waiting for transfers between devices: 147 us -> 152 us
    psum x1, waiting for transfers between devices: 91.7 us -> 25.2 us  [body(): lax.psum(grad_second.astype(jnp.bfloat16), 'batch').astype(jnp.float32)]
    all_gather x0 -> x1, waiting for transfers between devices: none -> 61.6 us  [body(): lax.all_gather(grad_first.astype(jnp.bfloat16), 'batch')]
    all_to_all x1, waiting for transfers between devices: 23.6 us -> 31.8 us  [body(): lax.all_to_all(grad_mixed, 'seq', split_axis=1, concat_axis=2, tiled=True)]
    all_to_all x1, starting transfers between devices: 16.9 us -> 9.76 us  [body(): lax.all_to_all(grad_mixed, 'seq', split_axis=1, concat_axis=2, tiled=True)]
    ppermute x2, starting transfers between devices: 13.8 us -> 8.58 us  [passed_along(): lax.ppermute(value, axis, [(source, source + steps) for source in range(i...]
    reduce_sum x0 -> x1, other arithmetic: none -> 4.93 us  [body(): jnp.sum(lax.all_gather(grad_first.astype(jnp.bfloat16), 'batch'), axis=0)]
  transfers between devices with their start and end apart: 5 -> 6, of which waited for: 5 -> 5; matrix products, arithmetic and copies ran while one was open for 12% -> 16% of each run, Pallas kernels for 0% -> 0%
where the time goes in v1:
time: 269 us; the launch traced here: 268 us
  waiting for transfers between devices  152 us (57%)
  starting transfers between devices  36.2 us (13%)
  local copies, waits for them, and re-layouts  26.7 us (10%)
  other arithmetic  21.5 us (8%)
  matrix products  17.8 us (7%)
  between operations  14.1 us (5%)
    all_gather x1, waiting for transfers between devices, body(): lax.all_gather(grad_first.astype(jnp.bfloat16), 'batch')  61.6 us
    all_to_all x1, waiting for transfers between devices, body(): lax.all_to_all(mixed, 'seq', split_axis=2, concat_axis=1, tiled=True)  32.6 us
    all_to_all x1, waiting for transfers between devices, body(): lax.all_to_all(grad_mixed, 'seq', split_axis=1, concat_axis=2, tiled=True)  31.8 us
    psum x1, waiting for transfers between devices, body(): lax.psum(grad_second.astype(jnp.bfloat16), 'batch').astype(jnp.float32)  25.2 us
    all_to_all x1, starting transfers between devices, body(): lax.all_to_all(mixed, 'seq', split_axis=2, concat_axis=1, tiled=True)  17.6 us
    all_to_all x1, starting transfers between devices, body(): lax.all_to_all(grad_mixed, 'seq', split_axis=1, concat_axis=2, tiled=True)  9.76 us
    ppermute x2, starting transfers between devices, passed_along(): lax.ppermute(value, axis, [(source, source + steps) for source in range(i...  8.58 us
  transfers between devices with their start and end apart: 6, of which 5 were waited for; matrix products, arithmetic and copies ran while one was open for 16% of the time, Pallas kernels for 0%

profile of v1, /device:TPU:1, one launch (start us, length us, event | category | flops | bytes accessed | tf_op | source)
XLA Modules:
  0.0 268.4 jit_solution(9329229375404878717)
XLA Ops:
  8.0 4.5 %collective-permute-start = (bf16[1,3,384]{2,1,0:T(4,128)(2,1)S(1)}, bf16[1,3,384]{2,1,0:T(4,128)(2,1)S(1)}, u32[]{:S(2)}, u32[]{:S(2)}) collective-permute-start(bf16[1,3,384]{2,1,0:T(4,128)(2,1)S(1)} %slice.47), channel_id=1, source_target_pairs={{0,1},{1,2},{2,3},{3,4},{4,5},{5,6},{6,7},{7,8},{8,9},{9,10},{10,1... | collective-permute-start | bytes 6920 | tf_op jit(solution)/shard_map/ppermute | solution.py:10
  12.5 0.9 slice_reduce_fusion.3
  13.4 1.7 maximum_convert_fusion
  15.1 3.1 %multiply_convert_fusion = (bf16[1,2048,384]{2,1,0:T(8,128)(2,1)S(1)}, f32[1,2048,384]{2,1,0:T(8,128)}) fusion(f32[1,2051,384]{2,1,0:T(8,128)S(1)} %maximum_convert_fusion, f32[384]{0:T(512)S(1)} %get-tuple-element.14, f32[384]{0:T(512)S(1)} %get-tuple-element.15, f32[384]{0:T(512)S(1)} %get-tuple-element.13, f32[384]{0:T(512)S(1)} %get-tuple-element.12), kind=kLoop, calls=%fused_computation.18 | loop fusion | flops 9437184 | bytes 17307648 | tf_op jit(solution)/shard_map/convert_element_type | solution.py:30
  18.3 1.2 copy-done.3
  19.4 2.3 fusion.10
  21.7 3.8 %copy.31 = bf16[1,4,512,384]{3,1,0,2:T(4,128)(2,1)} copy(bf16[1,4,512,384]{2,3,1,0:T(8,128)(2,1)} %fusion.10) | data formatting | bytes 3145728 | tf_op jit(solution)/shard_map/convert_element_type | solution.py:34
  25.5 17.6 %all-to-all-start.1 = ((bf16[1,4,512,384]{3,1,0,2:T(4,128)(2,1)}), bf16[1,4,512,384]{3,1,0,2:T(4,128)(2,1)}, u32[]{:S(2)}, u32[]{:S(2)}) async-start(bf16[1,4,512,384]{3,1,0,2:T(4,128)(2,1)} %copy.31), calls=%async_computation.1 | async-start | bytes 3145728 | tf_op jit(solution)/shard_map/all_to_all | solution.py:35
  43.1 4.2 %fusion.9 = bf16[1,512,4,384]{1,3,2,0:T(8,128)(2,1)} fusion(bf16[4,512,384]{2,1,0:T(8,128)(2,1)} %bitcast.40, bf16[4,512,512]{2,1,0:T(8,128)(2,1)} %param.8), kind=kOutput, calls=%fused_computation.29 | convolution fusion | flops 806092800 | bytes 5242880 | tf_op jit(solution)/shard_map/kmi,skmd->sikd/dot_general | solution.py:37
  47.3 3.8 %copy.25 = bf16[1,512,4,384]{3,2,0,1:T(4,128)(2,1)} copy(bf16[1,512,4,384]{1,3,2,0:T(8,128)(2,1)} %fusion.9) | data formatting | bytes 3145728 | tf_op jit(solution)/shard_map/convert_element_type | solution.py:39
  51.2 32.6 %all-to-all-done.1 = bf16[1,4,512,384]{3,1,0,2:T(4,128)(2,1)} async-done(((bf16[1,4,512,384]{3,1,0,2:T(4,128)(2,1)}), bf16[1,4,512,384]{3,1,0,2:T(4,128)(2,1)}, u32[]{:S(2)}, u32[]{:S(2)}) %all-to-all-start.1) | async-done | bytes 1572896 | tf_op jit(solution)/shard_map/all_to_all | solution.py:35
  83.7 9.8 %all-to-all-start = ((bf16[1,512,4,384]{3,2,0,1:T(4,128)(2,1)}), bf16[1,512,4,384]{3,2,0,1:T(4,128)(2,1)}, u32[]{:S(2)}, u32[]{:S(2)}) async-start(bf16[1,512,4,384]{3,2,0,1:T(4,128)(2,1)} %copy.25), calls=%async_computation | async-start | bytes 3145728 | tf_op jit(solution)/shard_map/all_to_all | solution.py:43
  93.6 3.1 %copy.32 = bf16[1,128,4,4,384]{4,2,1,3,0:T(4,128)(2,1)} copy(bf16[1,128,4,4,384]{4,2,3,1,0:T(4,128)(2,1)} %bitcast.14) | data formatting | bytes 3145728 | tf_op jit(solution)/shard_map/all_to_all | solution.py:35
  96.6 3.7 %reshape.110 = bf16[512,4,384]{2,0,1:T(8,128)(2,1)} reshape(bf16[1,128,4,4,384]{4,2,1,3,0:T(4,128)(2,1)} %copy.32) | data formatting | bytes 3145728 | tf_op jit(solution)/shard_map/reshape.23
  100.4 4.5 %convert_bitcast_fusion = bf16[4,512,512]{1,2,0:T(8,128)(2,1)} fusion(bf16[512,4,384]{2,0,1:T(8,128)(2,1)} %reshape.110, bf16[4,512,384]{2,1,0:T(8,128)(2,1)} %bitcast.41), kind=kOutput, calls=%fused_computation.21 | convolution fusion | flops 806354944 | bytes 5242880 | tf_op jit(solution)/shard_map/skmd,sikd->kmi/dot_general | solution.py:40
  105.1 31.8 %all-to-all-done = bf16[1,512,4,384]{3,2,0,1:T(4,128)(2,1)} async-done(((bf16[1,512,4,384]{3,2,0,1:T(4,128)(2,1)}), bf16[1,512,4,384]{3,2,0,1:T(4,128)(2,1)}, u32[]{:S(2)}, u32[]{:S(2)}) %all-to-all-start) | async-done | bytes 1572896 | tf_op jit(solution)/shard_map/all_to_all | solution.py:43
  136.8 2.1 copy.26
  139.0 1.1 copy-done.2
  140.1 2.6 convolution_convert_fusion
  142.8 4.2 %convolution_bitcast_fusion = f32[1,4,512,384]{2,3,1,0:T(8,128)} fusion(bf16[4,512,512]{2,1,0:T(8,128)(2,1)S(1)} %copy-done, bf16[4,512,384]{2,0,1:T(4,128)(2,1)} %bitcast.43), kind=kOutput, calls=%fused_computation.24 | convolution fusion | flops 805306368 | bytes 6815744 | tf_op jit(solution)/shard_map/ikj,sikd->sijd/dot_general | solution.py:44
  147.0 3.6 %copy.28 = f32[1,4,512,384]{3,2,1,0:T(8,128)} copy(f32[1,4,512,384]{2,3,1,0:T(8,128)} %convolution_bitcast_fusion) | data formatting | bytes 6291456 | tf_op jit(solution)/shard_map/ikj,sikd->sijd/transpose | solution.py:44
  150.6 4.0 %fusion.8 = bf16[1,2048,384]{2,1,0:T(8,128)(2,1)S(1)} fusion(f32[1,4,512,384]{3,2,1,0:T(8,128)} %copy.28, f32[1,2048,384]{2,1,0:T(8,128)} %get-tuple-element.17), kind=kLoop, calls=%fused_computation.17 | loop fusion | flops 7077888 | bytes 7864320 | tf_op jit(solution)/shard_map/convert_element_type | solution.py:47
  154.6 1.1 copy-done.1
  155.8 4.1 %collective-permute-start.1 = (bf16[1,3,384]{2,1,0:T(4,128)(2,1)S(1)}, bf16[1,3,384]{2,1,0:T(4,128)(2,1)S(1)}, u32[]{:S(2)}, u32[]{:S(2)}) collective-permute-start(bf16[1,3,384]{2,1,0:T(4,128)(2,1)S(1)} %slice.64), channel_id=1, source_target_pairs={{1,0},{2,1},{3,2},{4,3},{5,4},{6,5},{7,6},{8,7},{9,8},{10,9},{11,1... | collective-permute-start | bytes 6920 | tf_op jit(solution)/shard_map/ppermute | solution.py:10
  160.7 1.6 maximum_convert_fusion.1
  162.3 2.5 fusion.1
  164.8 25.2 %all-reduce.2.cloned.1.call-done = bf16[4,512,512]{1,2,0:T(8,128)(2,1)} async-done(((bf16[4,512,512]{1,2,0:T(8,128)(2,1)}), bf16[4,512,512]{1,2,0:T(8,128)(2,1)}) %all-reduce.2.cloned.1.call-update) | async-done | bytes 2097168 | tf_op jit(solution)/shard_map/psum | solution.py:60
  190.1 1.3 convert_convert_fusion
  191.4 1.3 copy.33
  192.7 61.6 %all-gather.3.cloned.1.call-done = bf16[8,512,512]{2,1,0:T(8,128)(2,1)} async-done(((bf16[4,512,512]{2,1,0:T(8,128)(2,1)}), bf16[8,512,512]{2,1,0:T(8,128)(2,1)}) %all-gather.3.cloned.1.call-update) | async-done | bytes 4194320 | tf_op jit(solution)/shard_map/all_gather | solution.py:57
  254.3 4.9 %reduce_sum.12 = bf16[4,512,512]{2,1,0:T(8,128)(2,1)} reduce(bf16[2,4,512,512]{3,2,1,0:T(8,128)(2,1)} %bitcast.46, bf16[]{:T(256)} %constant.4.clone.1), dimensions={0}, to_apply=%region_0.0 | reduce | flops 1048576 | bytes 6291458 | tf_op jit(solution)/shard_map/reduce_sum | solution.py:57
  259.3 2.3 convert_convert_fusion.1
  (15 shorter events, 2.0 us)
Async XLA Ops:
  7.2 12.3 %copy-start = (bf16[4,512,512]{2,1,0:T(8,128)(2,1)S(1)}, bf16[4,512,512]{2,1,0:T(8,128)(2,1)}, u32[]{:S(2)}) copy-start(bf16[4,512,512]{2,1,0:T(8,128)(2,1)} %param.7) | copy-start | bytes 6291460
  8.0 5.4 %collective-permute-start = (bf16[1,3,384]{2,1,0:T(4,128)(2,1)S(1)}, bf16[1,3,384]{2,1,0:T(4,128)(2,1)S(1)}, u32[]{:S(2)}, u32[]{:S(2)}) collective-permute-start(bf16[1,3,384]{2,1,0:T(4,128)(2,1)S(1)} %slice.47), channel_id=1, source_target_pairs={{0,1},{1,2},{2,3},{3,4},{4,5},{5,6},{6,7},{7,8},{8,9},{9,10},{10,1... | collective-permute-start | bytes 6920 | tf_op jit(solution)/shard_map/ppermute | solution.py:10
  18.3 1.2 copy-start.3
  25.5 58.2 %all-to-all-start.1 = ((bf16[1,4,512,384]{3,1,0,2:T(4,128)(2,1)}), bf16[1,4,512,384]{3,1,0,2:T(4,128)(2,1)}, u32[]{:S(2)}, u32[]{:S(2)}) async-start(bf16[1,4,512,384]{3,1,0,2:T(4,128)(2,1)} %copy.31), calls=%async_computation.1 | async-start | bytes 3145728 | tf_op jit(solution)/shard_map/all_to_all | solution.py:35
  83.7 53.1 %all-to-all-start = ((bf16[1,512,4,384]{3,2,0,1:T(4,128)(2,1)}), bf16[1,512,4,384]{3,2,0,1:T(4,128)(2,1)}, u32[]{:S(2)}, u32[]{:S(2)}) async-start(bf16[1,512,4,384]{3,2,0,1:T(4,128)(2,1)} %copy.25), calls=%async_computation | async-start | bytes 3145728 | tf_op jit(solution)/shard_map/all_to_all | solution.py:43
  93.5 96.6 %all-reduce.2.cloned.1.call-start = ((), (), s32[]{:S(2)}) async-start(), calls=%async_computation.2 | async-start | bytes 4194304 | tf_op jit(solution)/shard_map/psum | solution.py:60
  104.8 149.5 %all-gather.3.cloned.1.call-start = ((), (), s32[]{:S(2)}) async-start(), calls=%async_computation.3 | async-start | bytes 6291456 | tf_op jit(solution)/shard_map/all_gather | solution.py:57
  136.8 3.3 %copy-start.4 = (bf16[1,2048,384]{2,1,0:T(8,128)(2,1)S(1)}, bf16[1,2048,384]{2,1,0:T(8,128)(2,1)}, u32[]{:S(2)}) copy-start(bf16[1,2048,384]{2,1,0:T(8,128)(2,1)} %copy-done.3) | copy-start | bytes 4718596
  139.0 1.1 copy-start.2
  154.6 1.1 copy-start.1
  155.8 4.9 %collective-permute-start.1 = (bf16[1,3,384]{2,1,0:T(4,128)(2,1)S(1)}, bf16[1,3,384]{2,1,0:T(4,128)(2,1)S(1)}, u32[]{:S(2)}, u32[]{:S(2)}) collective-permute-start(bf16[1,3,384]{2,1,0:T(4,128)(2,1)S(1)} %slice.64), channel_id=1, source_target_pairs={{1,0},{2,1},{3,2},{4,3},{5,4},{6,5},{7,6},{8,7},{9,8},{10,9},{11,1... | collective-permute-start | bytes 6920 | tf_op jit(solution)/shard_map/ppermute | solution.py:10
Sparse Core Ops, SparseCore 0:
  105.0 85.0 all-reduce.1
  192.0 62.2 all-gather.2
